TPU v7x, 32 devices: a whole 2x2x4 slice. The times are simulated.
32 devices in a mesh: expert: 16 (over z, x, core), tensor: 2 (over y).
Axes of the slice: x: 2, y: 2, z: 4, core: 2. Of those that a mesh axis runs over, the one named last changes fastest.
Arguments:
- tokens: bfloat16 [256, 7168], P('expert', 'tensor'), may hold values from -6 to 6
- expert_ids: int32 [256, 8], P('expert'), may hold values from 0 to 7, as said below
- route_weights: float32 [256, 8], P('expert'), may hold values from 0.05 to 1
- gate_weight: bfloat16 [16, 512, 7168], P('expert', 'tensor'), may hold values from -0.0625 to 0.0625
- up_weight: bfloat16 [16, 512, 7168], P('expert', 'tensor'), may hold values from -0.0625 to 0.0625
- down_weight: bfloat16 [16, 512, 7168], P('expert', 'tensor'), may hold values from -0.1875 to 0.1875
Outputs:
- mixed: bfloat16 [256, 7168], P('expert', 'tensor')
Inputs may be any that keep to these rules, and one draw needn't show every extreme that they name: `expert_ids`: each row holds 8 different experts. One expert, the same for all tokens, is named by exactly 16 of the 16 tokens of every block of 16 consecutive tokens; every other expert by at most 16 tokens of a block.
All inputs are finite; a program needn't handle non-finite values.
Results may differ from a plain program's by a relative error of at most 0.015.
Values may be sent and summed in bfloat16 or wider, within the bound.
A program may use at most 64 MiB of HBM per device.

v0:
```python
import jax
import jax.numpy as jnp
from jax import lax
from jax.sharding import PartitionSpec as P


def rows_times(rows, weight):
    return lax.dot_general(
        rows, weight, (((1,), (1,)), ((), ())), preferred_element_type=jnp.float32
    )


def body(tokens, expert_ids, route_weights, gate_weight, up_weight, down_weight):
    devices_wide = lax.axis_size("expert")
    experts = devices_wide // 2
    tok_count = expert_ids.shape[0]
    per_token = expert_ids.shape[1]
    capacity = min(tok_count, tok_count * per_token // experts)
    slot_count = experts * capacity
    arrived_count = devices_wide * capacity
    expert_range = jnp.arange(experts, dtype=jnp.int32)
    onehot = jnp.sum(
        (expert_ids[:, :, None] == expert_range[None, None, :]).astype(jnp.int32), axis=1
    )
    earlier_count = jnp.cumsum(onehot, axis=0) - onehot
    slot_rank = jnp.take_along_axis(earlier_count, expert_ids, axis=1)
    slot_of = expert_ids * capacity + slot_rank
    slot_range = jnp.arange(slot_count, dtype=jnp.int32)
    select = jnp.any(slot_of[None, :, :] == slot_range[:, None, None], axis=2).astype(jnp.bfloat16)
    weight_gate = gate_weight[0]
    weight_up = up_weight[0]
    weight_out = down_weight[0]
    whole_rows = lax.all_gather(tokens, "tensor", axis=1, tiled=True)
    packed = jnp.dot(select, whole_rows, preferred_element_type=jnp.float32).astype(jnp.bfloat16)
    packed = packed.reshape(experts, capacity, whole_rows.shape[1])
    arrived = lax.all_to_all(
        jnp.repeat(packed, 2, axis=0), "expert", split_axis=0, concat_axis=0, tiled=True
    ).reshape(arrived_count, -1)
    gate_act = rows_times(arrived, weight_gate)
    up_act = rows_times(arrived, weight_up)
    hidden = (jax.nn.silu(gate_act) * up_act).astype(jnp.bfloat16)
    columns = lax.all_to_all(weight_out, "tensor", split_axis=1, concat_axis=0, tiled=True)
    unit_count = hidden.shape[1]
    shard_piece = lax.all_gather(hidden, "tensor", axis=1, tiled=True)
    groups = shard_piece.shape[1] // unit_count
    weight_rows = columns
    weight_rows = weight_rows.reshape(groups, unit_count, columns.shape[1])
    grouped = shard_piece.reshape(shard_piece.shape[0], groups, unit_count)
    group_terms = jnp.einsum(
        "rgf,gfd->grd", grouped, weight_rows, preferred_element_type=jnp.float32
    ).astype(jnp.bfloat16)
    group_terms = lax.optimization_barrier(group_terms)
    half_out = jnp.sum(group_terms.astype(jnp.float32), axis=0).astype(jnp.bfloat16)
    returned = lax.all_to_all(
        half_out.reshape(devices_wide, capacity, -1),
        "expert",
        split_axis=0,
        concat_axis=0,
        tiled=True,
    )
    returned = returned.reshape(experts, 2, capacity, -1).astype(jnp.float32)
    combined = (returned[:, 0] + returned[:, 1]).reshape(slot_count, -1)
    picked = combined[slot_of]
    mixed_out = jnp.sum(route_weights[:, :, None] * picked, axis=1)
    return mixed_out.astype(jnp.bfloat16)


def solution(mesh):
    placed = (
        P("expert", "tensor"),
        P("expert", None),
        P("expert", None),
        P("expert", "tensor", None),
        P("expert", "tensor", None),
        P("expert", "tensor", None),
    )
    return jax.shard_map(
        body, mesh=mesh, in_specs=placed, out_specs=P("expert", "tensor"), check_vma=False
    )
```

profile of v0, /device:TPU:11, one launch (start us, length us, event | category | flops | bytes accessed | tf_op | source)
XLA Modules:
  0.0 212.2 jit_solution(18340728612617636076)
XLA Ops:
  0.0 0.7 convert_reduce_fusion
  0.7 0.7 bitcast_or_fusion
  1.4 0.1 copy.24
  1.5 0.1 copy.26
  1.6 0.1 reshape.55
  1.7 0.0 copy-start.1
  1.7 0.0 copy-start
  1.7 1.3 gather_fusion.1
  3.0 0.1 reshape.58
  3.1 0.1 copy.27
  3.1 0.0 copy-done.1
  3.2 0.1 copy.28
  3.2 0.1 fusion.14
  3.3 0.0 copy-done
  3.3 4.7 %all_gather.6 = bf16[16,7168]{1,0:T(8,128)(2,1)S(1)} all-gather(bf16[16,3584]{1,0:T(8,128)(2,1)S(1)} %copy-done), channel_id=1, replica_groups=mesh['expert'=16,'tensor'=2] {'tensor'}, dimensions={1}, use_global_device_ids=true | all-gather | bytes 344064 | tf_op jit(solution)/shard_map/all_gather | solution.py:33
  8.0 0.7 convolution_convert_fusion
  8.7 2.3 %broadcast_in_dim.16 = bf16[8,2,16,7168]{3,2,1,0:T(8,128)(2,1)} broadcast(bf16[8,16,7168]{2,1,0:T(8,128)(2,1)S(1)} %bitcast.41), dimensions={0,2,3} | broadcast | bytes 5505024 | tf_op jit(solution)/shard_map/broadcast_in_dim | solution.py:37
  11.1 7.4 %all-to-all-start = ((bf16[16,16,7168]{2,1,0:T(8,128)(2,1)}), bf16[16,16,7168]{2,1,0:T(8,128)(2,1)}, u32[]{:S(2)}, u32[]{:S(2)}) async-start(bf16[16,16,7168]{2,1,0:T(8,128)(2,1)} %bitcast.39), calls=%async_computation | async-start | bytes 7340032 | tf_op jit(solution)/shard_map/all_to_all | solution.py:36
  18.4 5.9 %copy.29 = bf16[1,256,7168]{1,2,0:T(8,128)(2,1)} copy(bf16[1,256,7168]{2,1,0:T(8,128)(2,1)} %param.11) | data formatting | bytes 7340032 | tf_op args[5]
  24.4 6.0 %copy.30 = bf16[256,2,3584]{2,0,1:T(8,128)(2,1)} copy(bf16[256,2,3584]{0,2,1:T(8,128)(2,1)} %bitcast.38) | data formatting | bytes 7340032 | tf_op jit(solution)/shard_map/all_to_all | solution.py:42
  30.3 69.4 %all-to-all-done = bf16[16,16,7168]{2,1,0:T(8,128)(2,1)} async-done(((bf16[16,16,7168]{2,1,0:T(8,128)(2,1)}), bf16[16,16,7168]{2,1,0:T(8,128)(2,1)}, u32[]{:S(2)}, u32[]{:S(2)}) %all-to-all-start) | async-done | bytes 3670048 | tf_op jit(solution)/shard_map/all_to_all | solution.py:36
  99.7 5.5 %all-to-all-start.1 = ((bf16[256,2,3584]{2,0,1:T(8,128)(2,1)}), bf16[256,2,3584]{2,0,1:T(8,128)(2,1)}, u32[]{:S(2)}, u32[]{:S(2)}) async-start(bf16[256,2,3584]{2,0,1:T(8,128)(2,1)} %copy.30), calls=%async_computation.1 | async-start | bytes 7340032 | tf_op jit(solution)/shard_map/all_to_all | solution.py:42
  105.2 0.0 copy-start.3
  105.2 4.4 %fusion.3 = f32[256,256]{1,0:T(8,128)S(1)} fusion(bf16[256,7168]{1,0:T(8,128)(2,1)} %bitcast.3, bf16[1,256,7168]{2,1,0:T(8,128)(2,1)} %param.9), kind=kOutput, calls=%fused_computation.7 | convolution fusion | flops 939524096 | bytes 7602176 | tf_op jit(solution)/shard_map/dot_general | solution.py:8
  109.6 0.0 copy-done.3
  109.6 3.2 %fusion.9 = bf16[256,256]{1,0:T(8,128)(2,1)S(1)} fusion(bf16[256,7168]{1,0:T(8,128)(2,1)} %bitcast.3, bf16[1,256,7168]{2,1,0:T(8,128)(2,1)S(1)} %copy-done.3, f32[256,256]{1,0:T(8,128)S(1)} %fusion.3), kind=kOutput, calls=%fused_computation.13 | convolution fusion | flops 939917312 | bytes 7733248 | tf_op jit(solution)/shard_map/dot_general | solution.py:8
  112.8 36.8 %all_gather.7 = bf16[256,512]{1,0:T(8,128)(2,1)S(1)} all-gather(bf16[256,256]{1,0:T(8,128)(2,1)S(1)} %fusion.9), channel_id=1, replica_groups=mesh['expert'=16,'tensor'=2] {'tensor'}, dimensions={1}, use_global_device_ids=true | all-gather | bytes 393216 | tf_op jit(solution)/shard_map/all_gather | solution.py:44
  149.6 0.0 all-to-all-done.1
  149.6 5.0 %convolution_convert_fusion.1 = bf16[2,256,3584]{2,1,0:T(8,128)(2,1)} fusion(bf16[256,2,3584]{2,0,1:T(8,128)(2,1)} %all-to-all-done.1, bf16[32,2,8,256]{3,2,1,0:T(8,128)(2,1)S(1)} %bitcast.42), kind=kOutput, calls=%fused_computation.3 | convolution fusion | flops 941359104 | bytes 7602176 | tf_op jit(solution)/shard_map/rgf,gfd->grd/dot_general | solution.py:49
  154.6 0.0 copy-start.2
  154.6 4.4 %reduce_sum.31 = bf16[256,3584]{1,0:T(8,128)(2,1)} reduce(bf16[2,256,3584]{2,1,0:T(8,128)(2,1)} %convolution_convert_fusion.1, bf16[]{:T(256)} %constant.31.clone.1), dimensions={0}, to_apply=%region_3.4 | reduce | flops 917504 | bytes 5505026 | tf_op jit(solution)/shard_map/reduce_sum | solution.py:53
  159.0 5.6 %all-to-all-start.2 = ((bf16[16,16,3584]{2,1,0:T(8,128)(2,1)}), bf16[16,16,3584]{2,1,0:T(8,128)(2,1)S(1)}, u32[]{:S(2)}, u32[]{:S(2)}) async-start(bf16[16,16,3584]{2,1,0:T(8,128)(2,1)} %bitcast.8), calls=%async_computation.2 | async-start | bytes 3670016 | tf_op jit(solution)/shard_map/all_to_all | solution.py:54
  164.6 0.1 copy.32
  164.7 0.1 reshape.49
  164.8 0.0 copy-done.2
  164.8 0.1 copy.23
  164.9 41.6 %all-to-all-done.2 = bf16[16,16,3584]{2,1,0:T(8,128)(2,1)S(1)} async-done(((bf16[16,16,3584]{2,1,0:T(8,128)(2,1)}), bf16[16,16,3584]{2,1,0:T(8,128)(2,1)S(1)}, u32[]{:S(2)}, u32[]{:S(2)}) %all-to-all-start.2) | async-done | bytes 1835040 | tf_op jit(solution)/shard_map/all_to_all | solution.py:54
  206.4 0.4 convert.2
  206.9 0.2 slice_add_fusion
  207.1 2.4 %gather_fusion = f32[128,3584]{1,0:T(8,128)} fusion(f32[128,3584]{1,0:T(8,128)S(1)} %bitcast.37, s32[1024]{0:T(1024)S(1)} %pad_clamp_fusion), kind=kCustom, calls=%fused_computation | custom fusion | bytes 3670528 | tf_op jit(solution)/shard_map/gather | solution.py:63
  209.5 2.8 %fusion.5 = bf16[16,3584]{1,0:T(8,128)(2,1)} fusion(f32[128,3584]{1,0:T(8,128)} %gather_fusion, f32[16,8]{1,0:T(8,128)S(1)} %copy.23), kind=kLoop, calls=%fused_computation.11 | loop fusion | flops 860160 | bytes 1950208 | tf_op jit(solution)/shard_map/reduce_sum | solution.py:64
  (4 shorter events, 0.1 us)
Async XLA Ops:
  1.7 1.5 copy-start.1
  1.7 1.6 copy-start
  11.1 88.6 %all-to-all-start = ((bf16[16,16,7168]{2,1,0:T(8,128)(2,1)}), bf16[16,16,7168]{2,1,0:T(8,128)(2,1)}, u32[]{:S(2)}, u32[]{:S(2)}) async-start(bf16[16,16,7168]{2,1,0:T(8,128)(2,1)} %bitcast.39), calls=%async_computation | async-start | bytes 7340032 | tf_op jit(solution)/shard_map/all_to_all | solution.py:36
  99.7 49.9 %all-to-all-start.1 = ((bf16[256,2,3584]{2,0,1:T(8,128)(2,1)}), bf16[256,2,3584]{2,0,1:T(8,128)(2,1)}, u32[]{:S(2)}, u32[]{:S(2)}) async-start(bf16[256,2,3584]{2,0,1:T(8,128)(2,1)} %copy.30), calls=%async_computation.1 | async-start | bytes 7340032 | tf_op jit(solution)/shard_map/all_to_all | solution.py:42
  105.2 4.5 %copy-start.3 = (bf16[1,256,7168]{2,1,0:T(8,128)(2,1)S(1)}, bf16[1,256,7168]{2,1,0:T(8,128)(2,1)}, u32[]{:S(2)}) copy-start(bf16[1,256,7168]{2,1,0:T(8,128)(2,1)} %param.10) | copy-start | bytes 11010052
  154.6 10.2 %copy-start.2 = (f32[16,8]{0,1:T(8,128)S(1)}, f32[16,8]{0,1:T(8,128)}, u32[]{:S(2)}) copy-start(f32[16,8]{0,1:T(8,128)} %param.8) | copy-start | bytes 1540
  159.0 47.4 %all-to-all-start.2 = ((bf16[16,16,3584]{2,1,0:T(8,128)(2,1)}), bf16[16,16,3584]{2,1,0:T(8,128)(2,1)S(1)}, u32[]{:S(2)}, u32[]{:S(2)}) async-start(bf16[16,16,3584]{2,1,0:T(8,128)(2,1)} %bitcast.8), calls=%async_computation.2 | async-start | bytes 3670016 | tf_op jit(solution)/shard_map/all_to_all | solution.py:54
where the time goes:
time: 213 us; the launch traced here: 212 us
  waiting for transfers between devices  111 us (52%)
  blocking collectives  41.5 us (19%)
  local copies, waits for them, and re-layouts  18.6 us (9%)
  starting transfers between devices  18.5 us (9%)
  matrix products  13.3 us (6%)
  other arithmetic  9.36 us (4%)
    all_to_all x1, waiting for transfers between devices, body(): lax.all_to_all(jnp.repeat(packed, 2, axis=0), 'expert', split_axis=0, con...  69.4 us
    all_to_all x1, waiting for transfers between devices, body(): lax.all_to_all(half_out.reshape(devices_wide, capacity, -1), 'expert', sp...  41.6 us
    all_gather x1, blocking collectives, body(): shard_piece = lax.all_gather(hidden, 'tensor', axis=1, tiled=True)  36.8 us
    dot_general x2, matrix products, rows_times(): lax.dot_general(rows, weight, (((1,), (1,)), ((), ())), preferred_element...  7.63 us
    all_to_all x1, starting transfers between devices, body(): lax.all_to_all(jnp.repeat(packed, 2, axis=0), 'expert', split_axis=0, con...  7.38 us
    unnamed x10, local copies, waits for them, and re-layouts  6.01 us
    all_to_all x1, local copies, waits for them, and re-layouts, body(): lax.all_to_all(weight_out, 'tensor', split_axis=1, concat_axis=0, tiled=T...  5.95 us
    all_to_all x1, starting transfers between devices, body(): lax.all_to_all(half_out.reshape(devices_wide, capacity, -1), 'expert', sp...  5.63 us
  transfers between devices with their start and end apart: 3, of which 2 were waited for; matrix products, arithmetic and copies ran while one was open for 9% of the time, Pallas kernels for 0%

commit v1 on v0

--- a/solution.py
+++ b/solution.py
@@ -41,7 +41,11 @@
     hidden = (jax.nn.silu(gate_act) * up_act).astype(jnp.bfloat16)
     columns = lax.all_to_all(weight_out, "tensor", split_axis=1, concat_axis=0, tiled=True)
     unit_count = hidden.shape[1]
-    shard_piece = lax.all_gather(hidden, "tensor", axis=1, tiled=True)
+    shard_piece = jnp.roll(
+        jnp.concatenate([hidden, lax.ppermute(hidden, "tensor", [(0, 1), (1, 0)])], axis=1),
+        lax.axis_index("tensor") * hidden.shape[1],
+        axis=1,
+    )
     groups = shard_piece.shape[1] // unit_count
     weight_rows = columns
     weight_rows = weight_rows.reshape(groups, unit_count, columns.shape[1])

time: 213 us -> 214 us (level)
  blocking collectives: 41.5 us -> 4.69 us
  waiting for transfers between devices: 111 us -> 146 us
    all_gather x1 -> x0, blocking collectives: 36.8 us -> none  [body(): shard_piece = lax.all_gather(hidden, 'tensor', axis=1, tiled=True)]
    ppermute x0 -> x1, waiting for transfers between devices: none -> 35.3 us  [body(): lax.ppermute(hidden, 'tensor', [(0, 1), (1, 0)])]
  transfers between devices with their start and end apart: 3 -> 4, of which waited for: 2 -> 3; matrix products, arithmetic and copies ran while one was open for 9% -> 10% of each run, Pallas kernels for 0% -> 0%
where the time goes in v1:
time: 214 us; the launch traced here: 213 us
  waiting for transfers between devices  146 us (68%)
  starting transfers between devices  19.9 us (9%)
  local copies, waits for them, and re-layouts  18.5 us (9%)
  matrix products  13.3 us (6%)
  other arithmetic  10.5 us (5%)
  blocking collectives  4.69 us (2%)
    all_to_all x1, waiting for transfers between devices, body(): lax.all_to_all(jnp.repeat(packed, 2, axis=0), 'expert', split_axis=0, con...  69.4 us
    all_to_all x1, waiting for transfers between devices, body(): lax.all_to_all(half_out.reshape(devices_wide, capacity, -1), 'expert', sp...  41.6 us
    ppermute x1, waiting for transfers between devices, body(): lax.ppermute(hidden, 'tensor', [(0, 1), (1, 0)])  35.3 us
    dot_general x2, matrix products, rows_times(): lax.dot_general(rows, weight, (((1,), (1,)), ((), ())), preferred_element...  7.63 us
    all_to_all x1, starting transfers between devices, body(): lax.all_to_all(jnp.repeat(packed, 2, axis=0), 'expert', split_axis=0, con...  7.38 us
    unnamed x10, local copies, waits for them, and re-layouts  6.01 us
    all_to_all x1, local copies, waits for them, and re-layouts, body(): lax.all_to_all(weight_out, 'tensor', split_axis=1, concat_axis=0, tiled=T...  5.93 us
    all_to_all x1, starting transfers between devices, body(): lax.all_to_all(half_out.reshape(devices_wide, capacity, -1), 'expert', sp...  5.63 us
  transfers between devices with their start and end apart: 4, of which 3 were waited for; matrix products, arithmetic and copies ran while one was open for 10% of the time, Pallas kernels for 0%

profile of v1, /device:TPU:11, one launch (start us, length us, event | category | flops | bytes accessed | tf_op | source)
XLA Modules:
  0.0 213.3 jit_solution(10345774350778679764)
XLA Ops:
  0.0 0.7 convert_reduce_fusion
  0.7 0.7 bitcast_or_fusion
  1.4 0.1 copy.23
  1.5 0.1 copy.25
  1.6 0.1 reshape.55
  1.7 0.0 copy-start.1
  1.7 0.0 copy-start
  1.7 1.3 gather_fusion.1
  3.0 0.1 reshape.58
  3.1 0.1 copy.26
  3.1 0.0 copy-done.1
  3.2 0.1 copy.27
  3.2 0.1 fusion.15
  3.3 0.0 copy-done
  3.3 4.7 %all_gather.3 = bf16[16,7168]{1,0:T(8,128)(2,1)S(1)} all-gather(bf16[16,3584]{1,0:T(8,128)(2,1)S(1)} %copy-done), channel_id=1, replica_groups=mesh['expert'=16,'tensor'=2] {'tensor'}, dimensions={1}, use_global_device_ids=true | all-gather | bytes 344064 | tf_op jit(solution)/shard_map/all_gather | solution.py:33
  8.0 0.7 convolution_convert_fusion
  8.7 2.3 %broadcast_in_dim.16 = bf16[8,2,16,7168]{3,2,1,0:T(8,128)(2,1)} broadcast(bf16[8,16,7168]{2,1,0:T(8,128)(2,1)S(1)} %bitcast.39), dimensions={0,2,3} | broadcast | bytes 5505024 | tf_op jit(solution)/shard_map/broadcast_in_dim | solution.py:37
  11.0 7.4 %all-to-all-start = ((bf16[16,16,7168]{2,1,0:T(8,128)(2,1)}), bf16[16,16,7168]{2,1,0:T(8,128)(2,1)}, u32[]{:S(2)}, u32[]{:S(2)}) async-start(bf16[16,16,7168]{2,1,0:T(8,128)(2,1)} %bitcast.37), calls=%async_computation | async-start | bytes 7340032 | tf_op jit(solution)/shard_map/all_to_all | solution.py:36
  18.4 5.9 %copy.28 = bf16[1,256,7168]{1,2,0:T(8,128)(2,1)} copy(bf16[1,256,7168]{2,1,0:T(8,128)(2,1)} %param.11) | data formatting | bytes 7340032 | tf_op args[5]
  24.3 5.9 %copy.29 = bf16[256,2,3584]{2,0,1:T(8,128)(2,1)} copy(bf16[256,2,3584]{0,2,1:T(8,128)(2,1)} %bitcast.36) | data formatting | bytes 7340032 | tf_op jit(solution)/shard_map/all_to_all | solution.py:42
  30.2 69.4 %all-to-all-done = bf16[16,16,7168]{2,1,0:T(8,128)(2,1)} async-done(((bf16[16,16,7168]{2,1,0:T(8,128)(2,1)}), bf16[16,16,7168]{2,1,0:T(8,128)(2,1)}, u32[]{:S(2)}, u32[]{:S(2)}) %all-to-all-start) | async-done | bytes 3670048 | tf_op jit(solution)/shard_map/all_to_all | solution.py:36
  99.6 5.4 %all-to-all-start.1 = ((bf16[256,2,3584]{2,0,1:T(8,128)(2,1)}), bf16[256,2,3584]{2,0,1:T(8,128)(2,1)}, u32[]{:S(2)}, u32[]{:S(2)}) async-start(bf16[256,2,3584]{2,0,1:T(8,128)(2,1)} %copy.29), calls=%async_computation.1 | async-start | bytes 7340032 | tf_op jit(solution)/shard_map/all_to_all | solution.py:42
  105.0 0.0 copy-start.3
  105.0 4.4 %fusion.3 = f32[256,256]{0,1:T(8,128)S(1)} fusion(bf16[256,7168]{1,0:T(8,128)(2,1)} %bitcast.3, bf16[1,256,7168]{2,1,0:T(8,128)(2,1)} %param.9), kind=kOutput, calls=%fused_computation.7 | convolution fusion | flops 939524096 | bytes 7602176 | tf_op jit(solution)/shard_map/dot_general | solution.py:8
  109.5 0.0 copy-done.3
  109.5 3.2 %fusion.9 = bf16[256,256]{0,1:T(8,128)(2,1)S(1)} fusion(bf16[256,7168]{1,0:T(8,128)(2,1)} %bitcast.3, bf16[1,256,7168]{2,1,0:T(8,128)(2,1)S(1)} %copy-done.3, f32[256,256]{0,1:T(8,128)S(1)} %fusion.3), kind=kOutput, calls=%fused_computation.13 | convolution fusion | flops 939917312 | bytes 7733248 | tf_op jit(solution)/shard_map/dot_general | solution.py:8
  112.7 1.5 collective-permute-start
  114.2 35.3 %collective-permute-done = bf16[256,256]{0,1:T(8,128)(2,1)S(1)} collective-permute-done((bf16[256,256]{0,1:T(8,128)(2,1)S(1)}, bf16[256,256]{0,1:T(8,128)(2,1)S(1)}, u32[]{:S(2)}, u32[]{:S(2)}) %collective-permute-start) | collective-permute-done | bytes 131104 | tf_op jit(solution)/shard_map/ppermute | solution.py:45
  149.5 1.2 fusion.14
  150.7 0.0 all-to-all-done.1
  150.7 5.0 %convolution_convert_fusion.1 = bf16[2,256,3584]{2,1,0:T(8,128)(2,1)} fusion(bf16[256,2,256]{0,2,1:T(8,128)(2,1)S(1)} %bitcast.40, bf16[256,2,3584]{2,0,1:T(8,128)(2,1)} %all-to-all-done.1), kind=kOutput, calls=%fused_computation.3 | convolution fusion | flops 941359104 | bytes 7602176 | tf_op jit(solution)/shard_map/rgf,gfd->grd/dot_general | solution.py:53
  155.7 0.0 copy-start.2
  155.7 4.4 %reduce_sum.31 = bf16[256,3584]{1,0:T(8,128)(2,1)} reduce(bf16[2,256,3584]{2,1,0:T(8,128)(2,1)} %convolution_convert_fusion.1, bf16[]{:T(256)} %constant.58.clone.1), dimensions={0}, to_apply=%region_3.4 | reduce | flops 917504 | bytes 5505026 | tf_op jit(solution)/shard_map/reduce_sum | solution.py:57
  160.1 5.6 %all-to-all-start.2 = ((bf16[16,16,3584]{2,1,0:T(8,128)(2,1)}), bf16[16,16,3584]{2,1,0:T(8,128)(2,1)S(1)}, u32[]{:S(2)}, u32[]{:S(2)}) async-start(bf16[16,16,3584]{2,1,0:T(8,128)(2,1)} %bitcast.9), calls=%async_computation.2 | async-start | bytes 3670016 | tf_op jit(solution)/shard_map/all_to_all | solution.py:58
  165.7 0.1 copy.31
  165.8 0.1 reshape.49
  165.9 0.0 copy-done.2
  165.9 0.1 copy.22
  166.0 41.6 %all-to-all-done.2 = bf16[16,16,3584]{2,1,0:T(8,128)(2,1)S(1)} async-done(((bf16[16,16,3584]{2,1,0:T(8,128)(2,1)}), bf16[16,16,3584]{2,1,0:T(8,128)(2,1)S(1)}, u32[]{:S(2)}, u32[]{:S(2)}) %all-to-all-start.2) | async-done | bytes 1835040 | tf_op jit(solution)/shard_map/all_to_all | solution.py:58
  207.5 0.4 convert.2
  207.9 0.2 slice_add_fusion
  208.2 2.4 %gather_fusion = f32[128,3584]{1,0:T(8,128)} fusion(f32[128,3584]{1,0:T(8,128)S(1)} %bitcast.35, s32[1024]{0:T(1024)S(1)} %pad_clamp_fusion), kind=kCustom, calls=%fused_computation | custom fusion | bytes 3670528 | tf_op jit(solution)/shard_map/gather | solution.py:67
  210.6 2.8 %fusion.5 = bf16[16,3584]{1,0:T(8,128)(2,1)} fusion(f32[128,3584]{1,0:T(8,128)} %gather_fusion, f32[16,8]{1,0:T(8,128)S(1)} %copy.22), kind=kLoop, calls=%fused_computation.11 | loop fusion | flops 860160 | bytes 1950208 | tf_op jit(solution)/shard_map/reduce_sum | solution.py:68
  (4 shorter events, 0.1 us)
Async XLA Ops:
  1.7 1.5 copy-start.1
  1.7 1.6 copy-start
  11.0 88.6 %all-to-all-start = ((bf16[16,16,7168]{2,1,0:T(8,128)(2,1)}), bf16[16,16,7168]{2,1,0:T(8,128)(2,1)}, u32[]{:S(2)}, u32[]{:S(2)}) async-start(bf16[16,16,7168]{2,1,0:T(8,128)(2,1)} %bitcast.37), calls=%async_computation | async-start | bytes 7340032 | tf_op jit(solution)/shard_map/all_to_all | solution.py:36
  99.6 51.1 %all-to-all-start.1 = ((bf16[256,2,3584]{2,0,1:T(8,128)(2,1)}), bf16[256,2,3584]{2,0,1:T(8,128)(2,1)}, u32[]{:S(2)}, u32[]{:S(2)}) async-start(bf16[256,2,3584]{2,0,1:T(8,128)(2,1)} %copy.29), calls=%async_computation.1 | async-start | bytes 7340032 | tf_op jit(solution)/shard_map/all_to_all | solution.py:42
  105.0 4.5 %copy-start.3 = (bf16[1,256,7168]{2,1,0:T(8,128)(2,1)S(1)}, bf16[1,256,7168]{2,1,0:T(8,128)(2,1)}, u32[]{:S(2)}) copy-start(bf16[1,256,7168]{2,1,0:T(8,128)(2,1)} %param.10) | copy-start | bytes 11010052
  112.7 36.8 %collective-permute-start = (bf16[256,256]{0,1:T(8,128)(2,1)S(1)}, bf16[256,256]{0,1:T(8,128)(2,1)S(1)}, u32[]{:S(2)}, u32[]{:S(2)}) collective-permute-start(bf16[256,256]{0,1:T(8,128)(2,1)S(1)} %fusion.9), channel_id=1, source_target_pairs={{0,1},{1,0},{2,3},{3,2},{4,5},{5,4},{6,7},{7,6},{8,9},{9,8},{10,11... | collective-permute-start | bytes 393224 | tf_op jit(solution)/shard_map/ppermute | solution.py:45
  155.7 10.2 %copy-start.2 = (f32[16,8]{0,1:T(8,128)S(1)}, f32[16,8]{0,1:T(8,128)}, u32[]{:S(2)}) copy-start(f32[16,8]{0,1:T(8,128)} %param.8) | copy-start | bytes 1540
  160.1 47.4 %all-to-all-start.2 = ((bf16[16,16,3584]{2,1,0:T(8,128)(2,1)}), bf16[16,16,3584]{2,1,0:T(8,128)(2,1)S(1)}, u32[]{:S(2)}, u32[]{:S(2)}) async-start(bf16[16,16,3584]{2,1,0:T(8,128)(2,1)} %bitcast.9), calls=%async_computation.2 | async-start | bytes 3670016 | tf_op jit(solution)/shard_map/all_to_all | solution.py:58
